TPU v7x, 256 devices: a whole 4x4x8 slice. The times are simulated.
256 devices in a mesh: samp: 8 (over y, core), feat: 32 (over x, z).
Axes of the slice: x: 4, y: 4, z: 8, core: 2. Of those that a mesh axis runs over, the one named last changes fastest.
Arguments:
- samples: bfloat16 [8192, 16384], P('samp', 'feat'), may hold values from -8 to 8
- precision: float32 [128, 8, 128, 128], P('feat'), may hold values from -1.2 to 2
- col_blocks: int32 [128, 8], P('feat'), may hold values from -1 to 127, as said below
Outputs:
- updated: float32 [128, 8, 128, 128], P('feat')
Inputs may be any that keep to these rules, and one draw needn't show every extreme that they name: `col_blocks`: slot 0 of block row j holds j; the other column blocks of a row follow in increasing order, then -1 fills the empty slots. The pattern is symmetric: row j names c exactly when row c names j. Block row j lies on index j // 4 of feat; for two different such indices, at most one block row of the one names a column block of the other, and the block rows of one index name column blocks of at most 16 other indices.
All inputs are finite; a program needn't handle non-finite values.
Results may differ from a plain program's by a relative error of at most 0.0028.
Values may be sent and summed in bfloat16 or wider, within the bound.
A program may use at most 128 MiB of HBM per device.

v0:
```python
import jax
import jax.numpy as jnp
from jax import lax
from jax.sharding import PartitionSpec as P

ITERS = 3
step_size = 0.2
penalty = 0.25


def prox_step(current, gradient, keep_mask, on_diagonal):
    stepped = current - step_size * gradient
    shrunk = jnp.sign(stepped) * jnp.maximum(jnp.abs(stepped) - step_size * penalty, 0.0)
    rooted = 0.5 * (stepped + jnp.sqrt(stepped * stepped + 4.0 * step_size))
    return jnp.where(keep_mask, jnp.where(on_diagonal, rooted, shrunk), jnp.float32(0.0))


def mirror_outbound(flat_gram, send_slot, send_has):
    return jnp.where(
        send_has[:, None, None], jnp.take(flat_gram, send_slot, axis=0), jnp.float32(0.0)
    )


def mirror_inbound(inbound, flat_gram, holder, flat_local, remote):
    from_peer = jnp.take(inbound, holder, axis=0)
    from_self = jnp.take(flat_gram, flat_local, axis=0)
    return jnp.where(remote[:, :, None, None], from_peer, from_self)


def local(samples, precision, col_blocks):
    row_count = samples.shape[0]
    block_rows = precision.shape[0]
    slot_count = precision.shape[1]
    block_size = precision.shape[2]
    flat_count = block_rows * slot_count
    peer_count = lax.axis_size("feat")
    myself = lax.axis_index("feat")
    sample_total = row_count * lax.axis_size("samp")
    filled = col_blocks >= 0
    safe_cols = jnp.where(filled, col_blocks, 0)
    holder = safe_cols // block_rows
    locate = safe_cols % block_rows
    remote = filled & (holder != myself)
    xblocks = samples.reshape(row_count, block_rows, block_size)
    row_ids = myself * block_rows + jnp.arange(block_rows, dtype=jnp.int32)
    peer_ids = jnp.arange(peer_count, dtype=jnp.int32)
    slot_links = (holder[None] == peer_ids[:, None, None]) & remote[None]
    linked = jnp.any(slot_links, axis=2)
    has_link = jnp.any(linked, axis=1)
    source_row = jnp.argmax(linked, axis=1)
    outgoing = jnp.where(
        has_link[None, :, None], jnp.take(xblocks, source_row, axis=1), jnp.zeros((), samples.dtype)
    )
    flat_links = slot_links.reshape(peer_count, flat_count)
    send_slot = jnp.argmax(flat_links, axis=1)
    send_has = jnp.any(flat_links, axis=1)
    matching = col_blocks[locate] == row_ids[:, None, None]
    mate_slot = jnp.argmax(matching, axis=2)
    flat_local = locate * slot_count + mate_slot
    identity_mask = jnp.eye(block_size, dtype=bool)
    on_diagonal = (col_blocks == row_ids[:, None])[:, :, None, None] & identity_mask[None, None]
    keep_mask = filled[:, :, None, None]
    arrived = lax.all_to_all(outgoing, "feat", split_axis=1, concat_axis=1, tiled=True)
    joined = jnp.concatenate([arrived, xblocks], axis=1)
    source_index = jnp.where(remote, holder, peer_count + locate)
    stacked = jnp.take(joined, source_index, axis=1)
    current = jnp.where(keep_mask, precision, jnp.float32(0.0))
    weights = current.astype(jnp.bfloat16)
    for iteration in range(ITERS):
        running = jnp.einsum("rlkb,lkab->rla", stacked, weights, preferred_element_type=jnp.float32)
        projected = running.astype(jnp.bfloat16)
        partial_gram = jnp.einsum(
            "rla,rlkb->lkab", projected, stacked, preferred_element_type=jnp.float32
        )
        gram_blocks = lax.psum(partial_gram, "samp") / sample_total
        flat_gram = gram_blocks.reshape(flat_count, block_size, block_size)
        inbound = lax.all_to_all(
            mirror_outbound(flat_gram, send_slot, send_has),
            "feat",
            split_axis=0,
            concat_axis=0,
            tiled=True,
        )
        mirror = mirror_inbound(inbound, flat_gram, holder, flat_local, remote)
        gradient = 0.5 * (gram_blocks + jnp.swapaxes(mirror, 2, 3))
        current = prox_step(current, gradient, keep_mask, on_diagonal)
        weights = current.astype(jnp.bfloat16)
    return current


def solution(mesh):
    return jax.shard_map(
        local,
        mesh=mesh,
        in_specs=(P("samp", "feat"), P("feat", None, None, None), P("feat", None)),
        out_specs=P("feat", None, None, None),
        check_vma=False,
    )
```

profile of v0, /device:TPU:27, one launch (start us, length us, event | category | flops | bytes accessed | tf_op | source)
XLA Modules:
  0.0 750.6 jit_solution(2308110228360900354)
XLA Ops:
  8.0 1.3 gather_fusion.2
  9.3 0.8 iota_reduce_fusion
  10.1 0.8 compare_and_fusion
  11.5 1.5 copy.38
  13.7 4.8 gather_fusion
  18.4 7.6 %select_bitcast_fusion = bf16[1024,32,128]{2,0,1:T(8,128)(2,1)} fusion(bf16[32,1024,128]{2,1,0:T(8,128)(2,1)} %gather_fusion, pred[32]{0:T(512)(128)(4,1)S(1)} %get-tuple-element.13, pred[32]{0:T(512)(128)(4,1)S(1)} %compare_and_fusion.3), kind=kLoop, calls=%fused_computation.25 | loop fusion | flops 8388608 | bytes 16777280 | tf_op jit(solution)/shard_map/jit(_where)/select_n | solution.py:51
  26.0 11.2 %all-to-all-start = ((bf16[1024,32,128]{2,0,1:T(8,128)(2,1)}), bf16[1024,32,128]{2,0,1:T(8,128)(2,1)}, u32[]{:S(2)}, u32[]{:S(2)}) async-start(bf16[1024,32,128]{2,0,1:T(8,128)(2,1)} %select_bitcast_fusion), calls=%async_computation | async-start | bytes 16777216 | tf_op jit(solution)/shard_map/all_to_all | solution.py:63
  37.4 1.9 copy.37
  39.3 181.1 %all-to-all-done = bf16[1024,32,128]{2,0,1:T(8,128)(2,1)} async-done(((bf16[1024,32,128]{2,0,1:T(8,128)(2,1)}), bf16[1024,32,128]{2,0,1:T(8,128)(2,1)}, u32[]{:S(2)}, u32[]{:S(2)}) %all-to-all-start) | async-done | bytes 8388640 | tf_op jit(solution)/shard_map/all_to_all | solution.py:63
  220.5 8.9 %pad_maximum_fusion = bf16[1024,36,128]{2,0,1:T(8,128)(2,1)} fusion(bf16[1024,4,128]{2,0,1:T(8,128)(2,1)S(1)} %copy.39, bf16[1024,32,128]{2,0,1:T(8,128)(2,1)} %all-to-all-done), kind=kLoop, calls=%fused_computation.12 | loop fusion | flops 4718592 | bytes 18874368 | tf_op jit(solution)/shard_map/concatenate | solution.py:64
  229.4 8.6 %gather_fusion.1 = bf16[32,1024,128]{2,1,0:T(8,128)(2,1)} fusion(bf16[1024,36,128]{2,0,1:T(8,128)(2,1)} %pad_maximum_fusion, s32[1024]{0:T(1024)S(1)} %pad_clamp_fusion.4), kind=kCustom, calls=%fused_computation.10 | custom fusion | bytes 16777344 | tf_op jit(solution)/shard_map/jit(_take)/gather | solution.py:66
  238.0 11.3 %copy.41 = bf16[4,8,1024,128]{2,3,1,0:T(8,128)(2,1)} copy(bf16[4,8,1024,128]{3,2,1,0:T(8,128)(2,1)} %bitcast.129) | data formatting | bytes 16777216 | tf_op jit(solution)/shard_map/jit(_take)/gather | solution.py:66
  249.3 10.8 %fusion.23 = f32[4,8,128,128]{2,3,1,0:T(8,128)} fusion(bf16[4,8,1024,128]{2,3,1,0:T(8,128)(2,1)} %copy.41, pred[4,8]{1,0:T(4,128)(4,1)S(1)} %get-tuple-element.24, f32[4,8,128,128]{2,3,1,0:T(8,128)S(1)} %copy.37, pred[4,8]{1,0:T(4,128)(4,1)S(1)} %get-tuple-element.26), kind=kOutput, calls=%fused_computation.52 | convolution fusion | flops 2156920832 | bytes 12582976 | tf_op jit(solution)/shard_map/rla,rlkb->lkab/dot_general | solution.py:72
  260.3 0.7 iota_reduce_fusion.1
  261.1 80.3 %all-reduce.4.cloned.1.call-done = f32[4,8,128,128]{2,3,1,0:T(8,128)} async-done(((f32[4,8,128,128]{2,3,1,0:T(8,128)}), f32[4,8,128,128]{2,3,1,0:T(8,128)}) %all-reduce.4.cloned.1.call-update) | async-done | bytes 2097168 | tf_op jit(solution)/shard_map/psum | solution.py:75
  341.5 3.1 broadcast_multiply_fusion.2
  344.6 1.9 copy.45
  346.6 2.0 gather_fusion.3
  348.6 3.2 select_select_fusion.5
  351.7 9.6 %all-to-all-start.1 = ((f32[32,128,128]{2,1,0:T(8,128)}), f32[32,128,128]{2,1,0:T(8,128)}, u32[]{:S(2)}, u32[]{:S(2)}) async-start(f32[32,128,128]{2,1,0:T(8,128)} %select_select_fusion.5), calls=%async_computation.1 | async-start | bytes 4194304 | tf_op jit(solution)/shard_map/all_to_all | solution.py:77
  361.8 2.0 gather_fusion.5
  363.8 47.8 %all-to-all-done.1 = f32[32,128,128]{2,1,0:T(8,128)} async-done(((f32[32,128,128]{2,1,0:T(8,128)}), f32[32,128,128]{2,1,0:T(8,128)}, u32[]{:S(2)}, u32[]{:S(2)}) %all-to-all-start.1) | async-done | bytes 2097184 | tf_op jit(solution)/shard_map/all_to_all | solution.py:77
  411.7 3.6 gather_fusion.4
  415.2 5.9 fusion.12
  421.2 11.4 %fusion.28 = f32[4,8,128,128]{2,3,1,0:T(8,128)} fusion(bf16[4,8,1024,128]{2,3,1,0:T(8,128)(2,1)} %copy.41, pred[4,8]{1,0:T(4,128)(4,1)S(1)} %get-tuple-element.24, f32[4,8,128,128]{2,3,1,0:T(8,128)} %fusion.12), kind=kOutput, calls=%fused_computation.53 | convolution fusion | flops 2156920832 | bytes 12582944 | tf_op jit(solution)/shard_map/rla,rlkb->lkab/dot_general | solution.py:72
  432.6 68.1 %all-reduce.6.cloned.1.call-done = f32[4,8,128,128]{2,3,1,0:T(8,128)} async-done(((f32[4,8,128,128]{2,3,1,0:T(8,128)}), f32[4,8,128,128]{2,3,1,0:T(8,128)}) %all-reduce.6.cloned.1.call-update) | async-done | bytes 2097168 | tf_op jit(solution)/shard_map/psum | solution.py:75
  500.7 3.1 broadcast_multiply_fusion.1
  503.8 1.9 copy.50
  505.7 2.0 gather_fusion.6
  507.7 3.2 select_select_fusion.3
  510.9 9.6 %all-to-all-start.2 = ((f32[32,128,128]{2,1,0:T(8,128)}), f32[32,128,128]{2,1,0:T(8,128)}, u32[]{:S(2)}, u32[]{:S(2)}) async-start(f32[32,128,128]{2,1,0:T(8,128)} %select_select_fusion.3), calls=%async_computation.2 | async-start | bytes 4194304 | tf_op jit(solution)/shard_map/all_to_all | solution.py:77
  520.8 2.0 gather_fusion.8
  522.8 48.0 %all-to-all-done.2 = f32[32,128,128]{2,1,0:T(8,128)} async-done(((f32[32,128,128]{2,1,0:T(8,128)}), f32[32,128,128]{2,1,0:T(8,128)}, u32[]{:S(2)}, u32[]{:S(2)}) %all-to-all-start.2) | async-done | bytes 2097184 | tf_op jit(solution)/shard_map/all_to_all | solution.py:77
  570.9 3.6 gather_fusion.7
  574.5 6.5 fusion.13
  580.9 11.5 %fusion.33 = f32[4,8,128,128]{2,3,1,0:T(8,128)} fusion(bf16[4,8,1024,128]{2,3,1,0:T(8,128)(2,1)} %copy.41, pred[4,8]{1,0:T(4,128)(4,1)S(1)} %get-tuple-element.24, f32[4,8,128,128]{2,3,1,0:T(8,128)} %fusion.13), kind=kOutput, calls=%fused_computation.54 | convolution fusion | flops 2156920832 | bytes 12582944 | tf_op jit(solution)/shard_map/rla,rlkb->lkab/dot_general | solution.py:72
  592.5 68.1 %all-reduce.8.cloned.1.call-done = f32[4,8,128,128]{2,3,1,0:T(8,128)} async-done(((f32[4,8,128,128]{2,3,1,0:T(8,128)}), f32[4,8,128,128]{2,3,1,0:T(8,128)}) %all-reduce.8.cloned.1.call-update) | async-done | bytes 2097168 | tf_op jit(solution)/shard_map/psum | solution.py:75
  660.6 1.7 broadcast_multiply_fusion
  662.3 1.8 copy.55
  664.1 3.7 gather_fusion.9
  667.8 3.3 select_select_fusion.1
  671.1 9.6 %all-to-all-start.3 = ((f32[32,128,128]{2,1,0:T(8,128)}), f32[32,128,128]{2,1,0:T(8,128)}, u32[]{:S(2)}, u32[]{:S(2)}) async-start(f32[32,128,128]{2,1,0:T(8,128)} %select_select_fusion.1), calls=%async_computation.3 | async-start | bytes 4194304 | tf_op jit(solution)/shard_map/all_to_all | solution.py:77
  680.7 2.0 gather_fusion.11
  682.7 2.9 copy.56
  685.6 45.4 %all-to-all-done.3 = f32[32,128,128]{2,1,0:T(8,128)} async-done(((f32[32,128,128]{2,1,0:T(8,128)}), f32[32,128,128]{2,1,0:T(8,128)}, u32[]{:S(2)}, u32[]{:S(2)}) %all-to-all-start.3) | async-done | bytes 2097184 | tf_op jit(solution)/shard_map/all_to_all | solution.py:77
  731.0 3.6 gather_fusion.10
  734.6 6.5 fusion.14
  741.2 2.9 copy.57
  (39 shorter events, 4.0 us)
Async XLA Ops:
  26.0 194.5 %all-to-all-start = ((bf16[1024,32,128]{2,0,1:T(8,128)(2,1)}), bf16[1024,32,128]{2,0,1:T(8,128)(2,1)}, u32[]{:S(2)}, u32[]{:S(2)}) async-start(bf16[1024,32,128]{2,0,1:T(8,128)(2,1)} %select_bitcast_fusion), calls=%async_computation | async-start | bytes 16777216 | tf_op jit(solution)/shard_map/all_to_all | solution.py:63
  37.2 304.3 %all-reduce.4.cloned.1.call-start = ((), (), s32[]{:S(2)}) async-start(), calls=%async_computation.4 | async-start | bytes 4194304 | tf_op jit(solution)/shard_map/psum | solution.py:75
  39.3 210.0 %copy-start = (f32[4,8,128,128]{2,3,1,0:T(8,128)}, f32[4,8,128,128]{2,3,1,0:T(8,128)S(1)}, u32[]{:S(2)}) copy-start(f32[4,8,128,128]{2,3,1,0:T(8,128)S(1)} %copy.37) | copy-start | bytes 6291460
  351.7 59.9 %all-to-all-start.1 = ((f32[32,128,128]{2,1,0:T(8,128)}), f32[32,128,128]{2,1,0:T(8,128)}, u32[]{:S(2)}, u32[]{:S(2)}) async-start(f32[32,128,128]{2,1,0:T(8,128)} %select_select_fusion.5), calls=%async_computation.1 | async-start | bytes 4194304 | tf_op jit(solution)/shard_map/all_to_all | solution.py:77
  361.4 139.3 %all-reduce.6.cloned.1.call-start = ((), (), s32[]{:S(2)}) async-start(), calls=%async_computation.5 | async-start | bytes 4194304 | tf_op jit(solution)/shard_map/psum | solution.py:75
  363.8 51.4 %copy-start.1 = (f32[4,8,128,128]{2,3,1,0:T(8,128)S(1)}, f32[4,8,128,128]{2,3,1,0:T(8,128)}, u32[]{:S(2)}) copy-start(f32[4,8,128,128]{2,3,1,0:T(8,128)} %copy-done) | copy-start | bytes 6291460
  510.9 59.9 %all-to-all-start.2 = ((f32[32,128,128]{2,1,0:T(8,128)}), f32[32,128,128]{2,1,0:T(8,128)}, u32[]{:S(2)}, u32[]{:S(2)}) async-start(f32[32,128,128]{2,1,0:T(8,128)} %select_select_fusion.3), calls=%async_computation.2 | async-start | bytes 4194304 | tf_op jit(solution)/shard_map/all_to_all | solution.py:77
  520.6 140.0 %all-reduce.8.cloned.1.call-start = ((), (), s32[]{:S(2)}) async-start(), calls=%async_computation.6 | async-start | bytes 4194304 | tf_op jit(solution)/shard_map/psum | solution.py:75
  522.8 51.6 %copy-start.3 = (f32[4,8,128,128]{2,3,1,0:T(8,128)S(1)}, f32[4,8,128,128]{2,3,1,0:T(8,128)}, u32[]{:S(2)}) copy-start(f32[4,8,128,128]{2,3,1,0:T(8,128)} %all-reduce.6.cloned.1.call-done) | copy-start | bytes 6291460
  671.1 59.9 %all-to-all-start.3 = ((f32[32,128,128]{2,1,0:T(8,128)}), f32[32,128,128]{2,1,0:T(8,128)}, u32[]{:S(2)}, u32[]{:S(2)}) async-start(f32[32,128,128]{2,1,0:T(8,128)} %select_select_fusion.1), calls=%async_computation.3 | async-start | bytes 4194304 | tf_op jit(solution)/shard_map/all_to_all | solution.py:77
  685.6 49.0 %copy-start.2 = (f32[4,8,128,128]{2,3,1,0:T(8,128)S(1)}, f32[4,8,128,128]{2,3,1,0:T(8,128)}, u32[]{:S(2)}) copy-start(f32[4,8,128,128]{2,3,1,0:T(8,128)} %all-reduce.8.cloned.1.call-done) | copy-start | bytes 6291460
Sparse Core Ops, SparseCore 0:
  260.3 81.1 all-reduce.3
  432.7 67.9 all-reduce.5
  592.6 67.9 all-reduce.7
where the time goes:
time: 752 us; the launch traced here: 751 us
  waiting for transfers between devices  539 us (72%)
  local copies, waits for them, and re-layouts  66.4 us (9%)
  other arithmetic  57.6 us (8%)
  starting transfers between devices  40.7 us (5%)
  matrix products  33.7 us (4%)
  between operations  13.3 us (2%)
    psum x3, waiting for transfers between devices, local(): gram_blocks = lax.psum(partial_gram, 'samp') / sample_total  217 us
    all_to_all x1, waiting for transfers between devices, local(): lax.all_to_all(outgoing, 'feat', split_axis=1, concat_axis=1, tiled=True)  181 us
    all_to_all x3, waiting for transfers between devices, local(): lax.all_to_all(mirror_outbound(flat_gram, send_slot, send_has), 'feat', s...  141 us
    dot_general x3, matrix products, local(): jnp.einsum('rla,rlkb->lkab', projected, stacked, preferred_element_type=j...  33.7 us
    all_to_all x3, starting transfers between devices, local(): lax.all_to_all(mirror_outbound(flat_gram, send_slot, send_has), 'feat', s...  28.9 us
    gather x2, local copies, waits for them, and re-layouts, local(): stacked = jnp.take(joined, source_index, axis=1)  19.9 us
    select_n x3, other arithmetic, prox_step(): jnp.where(keep_mask, jnp.where(on_diagonal, rooted, shrunk), jnp.float32(...  19 us
  transfers between devices with their start and end apart: 7, of which 7 were waited for; matrix products, arithmetic and copies ran while one was open for 2% of the time, Pallas kernels for 0%

commit v1 on v0

--- a/solution.py
+++ b/solution.py
@@ -72,7 +72,7 @@
         partial_gram = jnp.einsum(
             "rla,rlkb->lkab", projected, stacked, preferred_element_type=jnp.float32
         )
-        gram_blocks = lax.psum(partial_gram, "samp") / sample_total
+        gram_blocks = jnp.sum(lax.all_gather(partial_gram, "samp"), axis=0) / sample_total
         flat_gram = gram_blocks.reshape(flat_count, block_size, block_size)
         inbound = lax.all_to_all(
             mirror_outbound(flat_gram, send_slot, send_has),

time: 752 us -> 845 us (1.12)
  waiting for transfers between devices: 539 us -> 584 us
  other arithmetic: 57.6 us -> 81.2 us
  local copies, waits for them, and re-layouts: 66.4 us -> 87.1 us
    all_gather x0 -> x3, waiting for transfers between devices: none -> 275 us  [local(): lax.all_gather(partial_gram, 'samp')]
    psum x3 -> x0, waiting for transfers between devices: 217 us -> none  [local(): gram_blocks = lax.psum(partial_gram, 'samp') / sample_total]
    reduce_sum x0 -> x3, other arithmetic: none -> 27.3 us  [local(): jnp.sum(lax.all_gather(partial_gram, 'samp'), axis=0) / sample_total]
    all_to_all x3, waiting for transfers between devices: 141 us -> 129 us  [local(): lax.all_to_all(mirror_outbound(flat_gram, send_slot, send_has), 'feat', s...]
    div x0 -> x3, local copies, waits for them, and re-layouts: none -> 8.82 us  [local(): jnp.sum(lax.all_gather(partial_gram, 'samp'), axis=0) / sample_total]
where the time goes in v1:
time: 845 us; the launch traced here: 838 us
  waiting for transfers between devices  584 us (69%)
  local copies, waits for them, and re-layouts  87.1 us (10%)
  other arithmetic  81.2 us (10%)
  starting transfers between devices  40.9 us (5%)
  matrix products  31.2 us (4%)
  between operations  13.3 us (2%)
    all_gather x3, waiting for transfers between devices, local(): lax.all_gather(partial_gram, 'samp')  275 us
    all_to_all x1, waiting for transfers between devices, local(): lax.all_to_all(outgoing, 'feat', split_axis=1, concat_axis=1, tiled=True)  181 us
    all_to_all x3, waiting for transfers between devices, local(): lax.all_to_all(mirror_outbound(flat_gram, send_slot, send_has), 'feat', s...  129 us
    dot_general x3, matrix products, local(): jnp.einsum('rla,rlkb->lkab', projected, stacked, preferred_element_type=j...  31.2 us
    all_to_all x3, starting transfers between devices, local(): lax.all_to_all(mirror_outbound(flat_gram, send_slot, send_has), 'feat', s...  28.9 us
    reduce_sum x3, other arithmetic, local(): jnp.sum(lax.all_gather(partial_gram, 'samp'), axis=0) / sample_total  27.3 us
    gather x2, local copies, waits for them, and re-layouts, local(): stacked = jnp.take(joined, source_index, axis=1)  20 us
    select_n x3, other arithmetic, prox_step(): jnp.where(keep_mask, jnp.where(on_diagonal, rooted, shrunk), jnp.float32(...  18.9 us
  transfers between devices with their start and end apart: 7, of which 7 were waited for; matrix products, arithmetic and copies ran while one was open for 2% of the time, Pallas kernels for 0%

profile of v1, /device:TPU:27, one launch (start us, length us, event | category | flops | bytes accessed | tf_op | source)
XLA Modules:
  0.0 838.3 jit_solution(2823277855494207585)
XLA Ops:
  13.7 4.8 gather_fusion
  18.4 7.6 select_bitcast_fusion
  26.0 11.2 %all-to-all-start = ((bf16[1024,32,128]{2,0,1:T(8,128)(2,1)}), bf16[1024,32,128]{2,0,1:T(8,128)(2,1)}, u32[]{:S(2)}, u32[]{:S(2)}) async-start(bf16[1024,32,128]{2,0,1:T(8,128)(2,1)} %select_bitcast_fusion), calls=%async_computation | async-start | bytes 16777216 | tf_op jit(solution)/shard_map/all_to_all | solution.py:63
  37.6 1.9 copy.78
  39.5 181.0 %all-to-all-done = bf16[1024,32,128]{2,0,1:T(8,128)(2,1)} async-done(((bf16[1024,32,128]{2,0,1:T(8,128)(2,1)}), bf16[1024,32,128]{2,0,1:T(8,128)(2,1)}, u32[]{:S(2)}, u32[]{:S(2)}) %all-to-all-start) | async-done | bytes 8388640 | tf_op jit(solution)/shard_map/all_to_all | solution.py:63
  220.5 9.0 %pad_maximum_fusion = bf16[1024,36,128]{2,0,1:T(8,128)(2,1)} fusion(bf16[1024,4,128]{2,0,1:T(8,128)(2,1)S(1)} %copy.80, bf16[1024,32,128]{2,0,1:T(8,128)(2,1)} %all-to-all-done), kind=kLoop, calls=%fused_computation.12 | loop fusion | flops 4718592 | bytes 18874368 | tf_op jit(solution)/shard_map/concatenate | solution.py:64
  229.4 8.7 %gather_fusion.1 = bf16[32,1024,128]{2,1,0:T(8,128)(2,1)} fusion(bf16[1024,36,128]{2,0,1:T(8,128)(2,1)} %pad_maximum_fusion, s32[1024]{0:T(1024)S(1)} %pad_clamp_fusion.4), kind=kCustom, calls=%fused_computation.10 | custom fusion | bytes 16777344 | tf_op jit(solution)/shard_map/jit(_take)/gather | solution.py:66
  238.1 11.3 %copy.82 = bf16[4,8,1024,128]{2,3,1,0:T(8,128)(2,1)} copy(bf16[4,8,1024,128]{3,2,1,0:T(8,128)(2,1)} %bitcast.132) | data formatting | bytes 16777216 | tf_op jit(solution)/shard_map/jit(_take)/gather | solution.py:66
  249.5 10.8 %fusion.23 = f32[4,8,128,128]{2,3,1,0:T(8,128)} fusion(bf16[4,8,1024,128]{2,3,1,0:T(8,128)(2,1)} %copy.82, pred[4,8]{1,0:T(4,128)(4,1)S(1)} %get-tuple-element.24, f32[4,8,128,128]{2,3,1,0:T(8,128)S(1)} %copy.78, pred[4,8]{1,0:T(4,128)(4,1)S(1)} %get-tuple-element.26), kind=kOutput, calls=%fused_computation.52 | convolution fusion | flops 2156920832 | bytes 12582976 | tf_op jit(solution)/shard_map/rla,rlkb->lkab/dot_general | solution.py:72
  260.2 2.9 copy.86
  264.1 97.1 %all-gather.7.cloned.1.call-done = f32[32,8,128,128]{3,2,1,0:T(8,128)} async-done(((f32[4,8,128,128]{3,2,1,0:T(8,128)}), f32[32,8,128,128]{3,2,1,0:T(8,128)}) %all-gather.7.cloned.1.call-update) | async-done | bytes 16777232 | tf_op jit(solution)/shard_map/all_gather | solution.py:75
  361.2 9.1 %reduce_sum.27 = f32[4,8,128,128]{3,2,1,0:T(8,128)} reduce(f32[8,4,8,128,128]{4,3,2,1,0:T(8,128)} %bitcast.139, f32[]{:T(128)} %constant.107.clone.1), dimensions={0}, to_apply=%region_3.4 | reduce | flops 3670016 | bytes 18874372 | tf_op jit(solution)/shard_map/reduce_sum | solution.py:75
  370.3 1.9 copy.120
  373.7 2.9 copy.88
  376.6 3.6 gather_fusion.3
  380.2 3.2 select_select_fusion.5
  383.4 9.6 %all-to-all-start.1 = ((f32[32,128,128]{2,1,0:T(8,128)}), f32[32,128,128]{2,1,0:T(8,128)}, u32[]{:S(2)}, u32[]{:S(2)}) async-start(f32[32,128,128]{2,1,0:T(8,128)} %select_select_fusion.5), calls=%async_computation.1 | async-start | bytes 4194304 | tf_op jit(solution)/shard_map/all_to_all | solution.py:77
  393.6 3.6 gather_fusion.5
  397.1 42.6 %all-to-all-done.1 = f32[32,128,128]{2,1,0:T(8,128)} async-done(((f32[32,128,128]{2,1,0:T(8,128)}), f32[32,128,128]{2,1,0:T(8,128)}, u32[]{:S(2)}, u32[]{:S(2)}) %all-to-all-start.1) | async-done | bytes 2097184 | tf_op jit(solution)/shard_map/all_to_all | solution.py:77
  439.8 3.6 gather_fusion.4
  443.4 5.9 fusion.12
  449.3 10.2 %fusion.28 = f32[4,8,128,128]{2,3,1,0:T(8,128)S(1)} fusion(bf16[4,8,1024,128]{2,3,1,0:T(8,128)(2,1)} %copy.82, pred[4,8]{1,0:T(4,128)(4,1)S(1)} %get-tuple-element.24, f32[4,8,128,128]{2,3,1,0:T(8,128)} %fusion.12), kind=kOutput, calls=%fused_computation.53 | convolution fusion | flops 2156920832 | bytes 12582944 | tf_op jit(solution)/shard_map/rla,rlkb->lkab/dot_general | solution.py:72
  459.5 1.9 copy.92
  461.5 88.9 %all-gather.9.cloned.1.call-done = f32[32,8,128,128]{3,2,1,0:T(8,128)} async-done(((f32[4,8,128,128]{3,2,1,0:T(8,128)}), f32[32,8,128,128]{3,2,1,0:T(8,128)}) %all-gather.9.cloned.1.call-update) | async-done | bytes 16777232 | tf_op jit(solution)/shard_map/all_gather | solution.py:75
  550.4 9.1 %reduce_sum.28 = f32[4,8,128,128]{3,2,1,0:T(8,128)} reduce(f32[8,4,8,128,128]{4,3,2,1,0:T(8,128)} %bitcast.141, f32[]{:T(128)} %constant.107.clone.1), dimensions={0}, to_apply=%region_7.10 | reduce | flops 3670016 | bytes 18874372 | tf_op jit(solution)/shard_map/reduce_sum | solution.py:75
  559.5 1.9 copy.121
  562.9 3.0 copy.94
  565.8 3.6 gather_fusion.6
  569.4 3.2 select_select_fusion.3
  572.6 9.6 %all-to-all-start.2 = ((f32[32,128,128]{2,1,0:T(8,128)}), f32[32,128,128]{2,1,0:T(8,128)}, u32[]{:S(2)}, u32[]{:S(2)}) async-start(f32[32,128,128]{2,1,0:T(8,128)} %select_select_fusion.3), calls=%async_computation.2 | async-start | bytes 4194304 | tf_op jit(solution)/shard_map/all_to_all | solution.py:77
  582.5 3.6 gather_fusion.8
  586.1 42.8 %all-to-all-done.2 = f32[32,128,128]{2,1,0:T(8,128)} async-done(((f32[32,128,128]{2,1,0:T(8,128)}), f32[32,128,128]{2,1,0:T(8,128)}, u32[]{:S(2)}, u32[]{:S(2)}) %all-to-all-start.2) | async-done | bytes 2097184 | tf_op jit(solution)/shard_map/all_to_all | solution.py:77
  628.9 3.7 gather_fusion.7
  632.6 6.5 fusion.13
  639.1 10.2 %fusion.33 = f32[4,8,128,128]{2,3,1,0:T(8,128)S(1)} fusion(bf16[4,8,1024,128]{2,3,1,0:T(8,128)(2,1)} %copy.82, pred[4,8]{1,0:T(4,128)(4,1)S(1)} %get-tuple-element.24, f32[4,8,128,128]{2,3,1,0:T(8,128)} %fusion.13), kind=kOutput, calls=%fused_computation.54 | convolution fusion | flops 2156920832 | bytes 12582944 | tf_op jit(solution)/shard_map/rla,rlkb->lkab/dot_general | solution.py:72
  649.3 1.9 copy.98
  651.2 88.9 %all-gather.11.cloned.1.call-done = f32[32,8,128,128]{3,2,1,0:T(8,128)} async-done(((f32[4,8,128,128]{3,2,1,0:T(8,128)}), f32[32,8,128,128]{3,2,1,0:T(8,128)}) %all-gather.11.cloned.1.call-update) | async-done | bytes 16777232 | tf_op jit(solution)/shard_map/all_gather | solution.py:75
  740.1 9.1 %reduce_sum.29 = f32[4,8,128,128]{3,2,1,0:T(8,128)} reduce(f32[8,4,8,128,128]{4,3,2,1,0:T(8,128)} %bitcast.140, f32[]{:T(128)} %constant.107.clone.1), dimensions={0}, to_apply=%region_8.11 | reduce | flops 3670016 | bytes 18874372 | tf_op jit(solution)/shard_map/reduce_sum | solution.py:75
  749.2 1.9 copy.122
  752.6 2.9 copy.100
  755.5 3.6 gather_fusion.9
  759.1 3.2 select_select_fusion.1
  762.3 9.6 %all-to-all-start.3 = ((f32[32,128,128]{2,1,0:T(8,128)}), f32[32,128,128]{2,1,0:T(8,128)}, u32[]{:S(2)}, u32[]{:S(2)}) async-start(f32[32,128,128]{2,1,0:T(8,128)} %select_select_fusion.1), calls=%async_computation.3 | async-start | bytes 4194304 | tf_op jit(solution)/shard_map/all_to_all | solution.py:77
  772.0 3.6 gather_fusion.11
  775.6 43.1 %all-to-all-done.3 = f32[32,128,128]{2,1,0:T(8,128)} async-done(((f32[32,128,128]{2,1,0:T(8,128)}), f32[32,128,128]{2,1,0:T(8,128)}, u32[]{:S(2)}, u32[]{:S(2)}) %all-to-all-start.3) | async-done | bytes 2097184 | tf_op jit(solution)/shard_map/all_to_all | solution.py:77
  818.7 3.6 gather_fusion.10
  822.3 6.5 fusion.14
  828.8 2.9 copy.101
  (41 shorter events, 13.5 us)
Async XLA Ops:
  26.0 194.5 %all-to-all-start = ((bf16[1024,32,128]{2,0,1:T(8,128)(2,1)}), bf16[1024,32,128]{2,0,1:T(8,128)(2,1)}, u32[]{:S(2)}, u32[]{:S(2)}) async-start(bf16[1024,32,128]{2,0,1:T(8,128)(2,1)} %select_bitcast_fusion), calls=%async_computation | async-start | bytes 16777216 | tf_op jit(solution)/shard_map/all_to_all | solution.py:63
  37.2 324.0 %all-gather.7.cloned.1.call-start = ((), (), s32[]{:S(2)}) async-start(), calls=%async_computation.4 | async-start | bytes 18874368 | tf_op jit(solution)/shard_map/all_gather | solution.py:75
  39.5 210.0 %copy-start = (f32[4,8,128,128]{2,3,1,0:T(8,128)}, f32[4,8,128,128]{2,3,1,0:T(8,128)S(1)}, u32[]{:S(2)}) copy-start(f32[4,8,128,128]{2,3,1,0:T(8,128)S(1)} %copy.78) | copy-start | bytes 6291460
  383.4 56.3 %all-to-all-start.1 = ((f32[32,128,128]{2,1,0:T(8,128)}), f32[32,128,128]{2,1,0:T(8,128)}, u32[]{:S(2)}, u32[]{:S(2)}) async-start(f32[32,128,128]{2,1,0:T(8,128)} %select_select_fusion.5), calls=%async_computation.1 | async-start | bytes 4194304 | tf_op jit(solution)/shard_map/all_to_all | solution.py:77
  393.1 157.3 %all-gather.9.cloned.1.call-start = ((), (), s32[]{:S(2)}) async-start(), calls=%async_computation.5 | async-start | bytes 18874368 | tf_op jit(solution)/shard_map/all_gather | solution.py:75
  572.6 56.3 %all-to-all-start.2 = ((f32[32,128,128]{2,1,0:T(8,128)}), f32[32,128,128]{2,1,0:T(8,128)}, u32[]{:S(2)}, u32[]{:S(2)}) async-start(f32[32,128,128]{2,1,0:T(8,128)} %select_select_fusion.3), calls=%async_computation.2 | async-start | bytes 4194304 | tf_op jit(solution)/shard_map/all_to_all | solution.py:77
  582.2 157.9 %all-gather.11.cloned.1.call-start = ((), (), s32[]{:S(2)}) async-start(), calls=%async_computation.6 | async-start | bytes 18874368 | tf_op jit(solution)/shard_map/all_gather | solution.py:75
  762.3 56.3 %all-to-all-start.3 = ((f32[32,128,128]{2,1,0:T(8,128)}), f32[32,128,128]{2,1,0:T(8,128)}, u32[]{:S(2)}, u32[]{:S(2)}) async-start(f32[32,128,128]{2,1,0:T(8,128)} %select_select_fusion.1), calls=%async_computation.3 | async-start | bytes 4194304 | tf_op jit(solution)/shard_map/all_to_all | solution.py:77
Sparse Core Ops, SparseCore 0:
  263.3 97.8 all-gather.6
  461.6 88.7 all-gather.8
  651.3 88.7 all-gather.10
